TPU v7x, 1024 devices: a whole 8x8x8 slice. The times are simulated.
1024 devices in a mesh: band: 32 (over x_hi, z, core), dom: 32 (over x_lo, y).
Axes of the slice: x: 8 (x_hi: 2, x_lo: 4; x = x_hi * 4 + x_lo), y: 8, z: 8, core: 2. Of those that a mesh axis runs over, the one named last changes fastest.
Arguments:
- orbitals: bfloat16 [2048, 196608], P('band', 'dom'), may hold values from -6 to 6
- rotation: bfloat16 [2048, 256], P('band'), may hold values from -0.375 to 0.375
- projectors: bfloat16 [32, 16, 196608], P(None, None, 'dom'), may hold values from -0.078125 to 0.078125
- coupling: float32 [512, 16, 16], P('dom'), may hold values from -5 to 5
- slot_atom: int32 [32, 32], replicated, may hold values from 0 to 511, as said below
Outputs:
- updated_orbitals: bfloat16 [2048, 196608], P('band', 'dom')
Inputs may be any that keep to these rules, and one draw needn't show every extreme that they name: `slot_atom`: the atoms of one row are distinct. Atom a is owned by domain a // 16. A row names at most 4 atoms of any one owner; domain 32 - 1 is named exactly 4 times by every row. Other owners are named between 0 and 4 times, unevenly.
All inputs are finite; a program needn't handle non-finite values.
Results may differ from a plain program's by a relative error of at most 0.0057.
Values may be sent and summed in bfloat16 or wider, within the bound.
A program may use at most 32 MiB of HBM per device.

v0:
```python
import jax
import jax.numpy as jnp
from jax import lax
from jax.sharding import PartitionSpec as P


def passed_along(block, axis, distance):
    devices = range(lax.axis_size(axis))
    route = [((i - distance) % len(devices), i) for i in devices]
    return lax.ppermute(block, axis, route)


def couple_atoms(coupling, summed, proj_count):
    atom_count = summed.shape[0]
    shaped = summed.reshape(atom_count, proj_count, -1)
    coupled = jnp.einsum("apq,aqo->apo", coupling, shaped, precision=lax.Precision.HIGHEST)
    return coupled.astype(jnp.bfloat16).reshape(atom_count, -1)


def on_device(orbitals, rotation, projectors, coupling, slot_atom):
    width = orbitals.shape[0]
    stop_count = rotation.shape[1] // width
    running = jnp.dot(rotation[:, :width], orbitals, preferred_element_type=jnp.float32)
    moving = orbitals
    for stop_index in range(1, stop_count):
        moving = passed_along(moving, "band", 1)
        running = running + jnp.dot(
            rotation[:, stop_index * width : (stop_index + 1) * width],
            moving,
            preferred_element_type=jnp.float32,
        )
    rotated = running.astype(jnp.bfloat16)
    slot_count = projectors.shape[0]
    proj_count = projectors.shape[1]
    partial_value = jnp.einsum(
        "kpg,og->kpo", projectors, rotated, preferred_element_type=jnp.float32
    ).reshape(slot_count, -1)
    domain_index = lax.axis_index("dom")
    domain_count = lax.axis_size("dom")
    owned = coupling.shape[0]
    own_atoms = lax.dynamic_index_in_dim(slot_atom, domain_index, 0, keepdims=False)
    atom_total = owned * domain_count
    onehot = (own_atoms[:, None] == jnp.arange(atom_total, dtype=jnp.int32)[None, :]).astype(
        jnp.float32
    )
    spread = jnp.dot(onehot.T, partial_value, precision=lax.Precision.HIGHEST)
    summed = lax.psum_scatter(spread, "dom", scatter_dimension=0, tiled=True)
    coupled = couple_atoms(coupling, summed, proj_count)
    gathered = lax.all_gather(coupled, "dom", axis=0, tiled=True)
    returned = jnp.take(gathered, own_atoms, axis=0)
    applied = jnp.einsum(
        "kpg,kpo->og",
        projectors,
        returned.reshape(slot_count, proj_count, width),
        preferred_element_type=jnp.float32,
    )
    return (rotated.astype(jnp.float32) + applied).astype(jnp.bfloat16)


def solution(mesh):
    in_specs = (P("band", "dom"), P("band", None), P(None, None, "dom"), P("dom", None, None), P())
    out_specs = P("band", "dom")
    return jax.shard_map(
        on_device, mesh=mesh, in_specs=in_specs, out_specs=out_specs, check_vma=False
    )
```

profile of v0, /device:TPU:16, one launch (start us, length us, event | category | flops | bytes accessed | tf_op | source)
XLA Modules:
  0.0 432.8 jit_solution(1265770757350118671)
XLA Ops:
  6.5 0.0 copy-start
  6.5 0.0 copy-start.2
  6.5 0.0 reduce-scatter.2.cloned.1.call-start
  6.5 2.0 collective-permute-start
  8.6 34.8 %collective-permute-done = bf16[64,6144]{1,0:T(8,128)(2,1)S(1)} collective-permute-done((bf16[64,6144]{1,0:T(8,128)(2,1)}, bf16[64,6144]{1,0:T(8,128)(2,1)S(1)}, u32[]{:S(2)}, u32[]{:S(2)}) %collective-permute-start) | collective-permute-done | bytes 786464 | tf_op jit(solution)/shard_map/ppermute | solution.py:10
  43.4 1.9 collective-permute-start.1
  45.3 26.0 %collective-permute-done.1 = bf16[64,6144]{1,0:T(8,128)(2,1)} collective-permute-done((bf16[64,6144]{1,0:T(8,128)(2,1)S(1)}, bf16[64,6144]{1,0:T(8,128)(2,1)}, u32[]{:S(2)}, u32[]{:S(2)}) %collective-permute-start.1) | collective-permute-done | bytes 786464 | tf_op jit(solution)/shard_map/ppermute | solution.py:10
  71.2 1.9 collective-permute-start.2
  73.2 1.5 fusion.18
  74.7 0.7 compare_and_fusion
  75.4 0.0 copy-done.2
  75.4 0.4 convolution_add_fusion.2
  75.8 0.0 copy-start.1
  75.8 1.6 convolution_add_fusion.1
  77.4 21.7 %collective-permute-done.2 = bf16[64,6144]{1,0:T(8,128)(2,1)S(1)} collective-permute-done((bf16[64,6144]{1,0:T(8,128)(2,1)}, bf16[64,6144]{1,0:T(8,128)(2,1)S(1)}, u32[]{:S(2)}, u32[]{:S(2)}) %collective-permute-start.2) | collective-permute-done | bytes 786464 | tf_op jit(solution)/shard_map/ppermute | solution.py:10
  99.1 0.4 fusion
  99.5 0.0 copy-done.1
  99.6 4.2 fusion.4
  103.7 0.2 copy.10
  103.9 0.1 reshape.51
  104.0 2.4 fusion.13
  106.5 0.0 reduce-scatter.2.cloned.1.call-update
  106.5 0.0 all-gather.2.cloned.1.call-start
  106.5 155.4 %reduce-scatter.2.cloned.1.call-done = f32[16,1024]{1,0:T(8,128)} async-done(((f32[512,1024]{1,0:T(8,128)}), f32[16,1024]{1,0:T(8,128)}) %reduce-scatter.2.cloned.1.call-update) | async-done | bytes 65552 | tf_op jit(solution)/shard_map/reduce_scatter | solution.py:47
  261.9 0.9 reshape.52
  262.8 0.0 copy-done
  262.9 0.3 fusion.7
  263.1 0.7 reshape.53
  263.8 0.0 all-gather.2.cloned.1.call-update
  263.9 0.7 fusion.20
  264.6 151.8 %all-gather.2.cloned.1.call-done = bf16[512,1024]{1,0:T(8,128)(2,1)} async-done(((bf16[16,1024]{1,0:T(8,128)(2,1)}), bf16[512,1024]{1,0:T(8,128)(2,1)}) %all-gather.2.cloned.1.call-update) | async-done | bytes 1048592 | tf_op jit(solution)/shard_map/all_gather | solution.py:49
  416.3 2.0 gather_fusion
  418.4 0.1 gather.7
  418.5 7.4 %add_convert_fusion = bf16[64,6144]{1,0:T(8,128)(2,1)} fusion(bf16[64,6144]{1,0:T(8,128)(2,1)S(1)} %fusion, bf16[32,16,6144]{2,1,0:T(8,128)(2,1)} %param.7, bf16[32,16,64]{2,1,0:T(8,128)(2,1)S(1)} %gather.7, pred[32]{0:T(512)(128)(4,1)S(1)} %get-tuple-element.5), kind=kOutput, calls=%fused_computation.9 | convolution fusion | flops 403865600 | bytes 7929888 | tf_op jit(solution)/shard_map/kpg,kpo->og/dot_general | solution.py:51
  (1 shorter events, 0.0 us)
Async XLA Ops:
  6.5 256.3 %copy-start = (f32[16,16,16]{2,1,0:T(8,128)S(1)}, f32[16,16,16]{2,1,0:T(8,128)}, u32[]{:S(2)}) copy-start(f32[16,16,16]{2,1,0:T(8,128)} %param.8) | copy-start | bytes 49156
  6.5 68.8 %copy-start.2 = (bf16[64,256]{1,0:T(8,128)(2,1)S(1)}, bf16[64,256]{1,0:T(8,128)(2,1)}, u32[]{:S(2)}) copy-start(bf16[64,256]{1,0:T(8,128)(2,1)} %param.6) | copy-start | bytes 98308
  6.5 255.4 %reduce-scatter.2.cloned.1.call-start = ((), (), s32[]{:S(2)}) async-start(), calls=%async_computation.1 | async-start | bytes 2162688 | tf_op jit(solution)/shard_map/reduce_scatter | solution.py:47
  6.5 36.8 %collective-permute-start = (bf16[64,6144]{1,0:T(8,128)(2,1)}, bf16[64,6144]{1,0:T(8,128)(2,1)S(1)}, u32[]{:S(2)}, u32[]{:S(2)}) collective-permute-start(bf16[64,6144]{1,0:T(8,128)(2,1)} %param.5), channel_id=1, source_target_pairs={{992,0},{0,32},{32,64},{64,96},{96,128},{128,160},{160,192},{192,2... | collective-permute-start | bytes 2359304 | tf_op jit(solution)/shard_map/ppermute | solution.py:10
  43.4 27.9 %collective-permute-start.1 = (bf16[64,6144]{1,0:T(8,128)(2,1)S(1)}, bf16[64,6144]{1,0:T(8,128)(2,1)}, u32[]{:S(2)}, u32[]{:S(2)}) collective-permute-start(bf16[64,6144]{1,0:T(8,128)(2,1)S(1)} %collective-permute-done), channel_id=1, source_target_pairs={{992,0},{0,32},{32,64},{64,96},{96,128},{128,160},{160,192},{192,2... | collective-permute-start | bytes 2359304 | tf_op jit(solution)/shard_map/ppermute | solution.py:10
  71.2 27.9 %collective-permute-start.2 = (bf16[64,6144]{1,0:T(8,128)(2,1)}, bf16[64,6144]{1,0:T(8,128)(2,1)S(1)}, u32[]{:S(2)}, u32[]{:S(2)}) collective-permute-start(bf16[64,6144]{1,0:T(8,128)(2,1)} %collective-permute-done.1), channel_id=1, source_target_pairs={{992,0},{0,32},{32,64},{64,96},{96,128},{128,160},{160,192},{192,2... | collective-permute-start | bytes 2359304 | tf_op jit(solution)/shard_map/ppermute | solution.py:10
  75.8 23.8 %copy-start.1 = (bf16[32,16,6144]{2,1,0:T(8,128)(2,1)S(1)}, bf16[32,16,6144]{2,1,0:T(8,128)(2,1)}, u32[]{:S(2)}) copy-start(bf16[32,16,6144]{2,1,0:T(8,128)(2,1)} %param.7) | copy-start | bytes 18874372
  106.5 309.9 %all-gather.2.cloned.1.call-start = ((), (), s32[]{:S(2)}) async-start(), calls=%async_computation.2 | async-start | bytes 1081344 | tf_op jit(solution)/shard_map/all_gather | solution.py:49
Sparse Core Ops, SparseCore 0:
  106.6 155.2 reduce-scatter.1
  264.9 151.3 all-gather.1
where the time goes:
time: 433 us
  waiting for transfers between devices  390 us (90%)
  matrix products  18.2 us (4%)
  between operations  13.5 us (3%)
  starting transfers between devices  5.9 us (1%)
    reduce_scatter x1, waiting for transfers between devices, on_device(): summed = lax.psum_scatter(spread, 'dom', scatter_dimension=0, tiled=True)  155 us
    all_gather x1, waiting for transfers between devices, on_device(): gathered = lax.all_gather(coupled, 'dom', axis=0, tiled=True)  152 us
    ppermute x3, waiting for transfers between devices, passed_along(): return lax.ppermute(block, axis, route)  82.4 us
  transfers between devices with their start and end apart: 5, of which 5 were waited for; matrix products, arithmetic and copies ran while one was open for 1% of the time, Pallas kernels for 0%

commit v1 on v0

v1 whole, which is shorter than its diff:
```python
import functools

import jax
import jax.numpy as jnp
from jax import lax
from jax.experimental import pallas as pl
from jax.experimental.pallas import tpu as pltpu
from jax.sharding import PartitionSpec as P

MESH = pl.DeviceIdType.MESH
ANY = pl.ANY
VMEM = pltpu.VMEM
F32 = jnp.float32
BF16 = jnp.bfloat16
HIGH = lax.Precision.HIGHEST

CHUNKS = 6
COLS, ROWS = 4, 8


def dot(a, b, dims, precision=None):
    return lax.dot_general(a, b, (dims, ((), ())), precision=precision, preferred_element_type=F32)


def kernel(
    orb_hbm, rot, proj_hbm, coup, slot, out_hbm,
    xs, pj, q32, g, cg, xsend, xrecv, csend, crecv, sb, kr, bd, crow, s32, ct, outv,
    orb_sem, proj_sem, out_sem,
    link_s, link_r, pair_s, pair_r, own_s, own_r, third_s, third_r,
    y_s, y_r, cy_s, cy_r, x_s, x_r, cx_s, cx_r,
):
    band = lax.axis_index("band")
    dom = lax.axis_index("dom")
    n_band = lax.axis_size("band")
    core = lax.rem(band, 2)
    col, row = dom // ROWS, lax.rem(dom, ROWS)
    width = rot.shape[0]
    cw = xs.shape[2]
    n_slot = slot.shape[1]
    n_proj = coup.shape[1] // 16

    first = band - core
    nxt = lax.rem(first + 2, n_band)
    prv = lax.rem(first + n_band - 2, n_band)
    partner = (first + 1 - core, dom)
    ahead = (nxt + core, dom)
    ahead0 = (nxt, dom)
    up = (band, col * ROWS + lax.rem(row + 1, ROWS))
    down = (band, col * ROWS + lax.rem(row + ROWS - 1, ROWS))

    def across(k):
        return (band, lax.rem(col + k, COLS) * ROWS + row)

    for j in range(CHUNKS):
        pltpu.make_async_copy(orb_hbm.at[:, pl.ds(j * cw, cw)], xs.at[j, pl.ds(0, width)], orb_sem.at[j]).start()
    for j in range(CHUNKS):
        pltpu.make_async_copy(proj_hbm.at[:, pl.ds(j * cw, cw)], pj.at[j], proj_sem.at[j]).start()

    barrier = pltpu.get_barrier_semaphore()
    friends = [
        partner, (nxt + core, dom), (nxt + 1 - core, dom), (prv + core, dom), (prv + 1 - core, dom),
        up, down, across(1), across(2), across(3),
    ]
    for friend in friends:
        pl.semaphore_signal(barrier, inc=1, device_id=friend, device_id_type=MESH)
    pl.semaphore_wait(barrier, len(friends))

    def remote(src, dst, s, r, to):
        return pltpu.make_async_remote_copy(
            src_ref=src, dst_ref=dst, send_sem=s, recv_sem=r, device_id=to, device_id_type=MESH
        )

    half = width // 2

    def link(j, part):
        return remote(part(0, 0, 1), part(2, 0, 1), link_s.at[j], link_r.at[j], ahead)

    def own(j, part):
        return remote(part(0, 0, 1), part(1, 0, 1), own_s.at[j], own_r.at[j], partner)

    def pair(j, part, c):
        return remote(part(2, 0, 1), part(3 if c == 0 else 1, 0, 1), pair_s.at[j], pair_r.at[j], partner)

    def third(j, part, c):
        return remote(part(1 + c, c, 2), part(3, c, 2), third_s.at[j], third_r.at[j, c], ahead0)

    def start_item(j, part):
        link(j, part).start()

        @pl.when(core == 0)
        def _():
            own(j, part).start()

    def forward_item(j, part):
        link(j, part).wait_recv()

        @pl.when(core == 0)
        def _():
            pair(j, part, 0).start()
            pair(j, part, 1).wait_recv()
            third(j, part, 0).start()

        @pl.when(core == 1)
        def _():
            pair(j, part, 1).start()
            third(j, part, 1).start()

    def finish_item(j, part):
        @pl.when(core == 0)
        def _():
            third(j, part, 0).wait_recv()
            third(j, part, 1).wait_recv()

        @pl.when(core == 1)
        def _():
            own(j, part).wait_recv()
            pair(j, part, 0).wait_recv()

    def drain_item(j, part):
        link(j, part).wait_send()

        @pl.when(core == 0)
        def _():
            own(j, part).wait_send()
            pair(j, part, 0).wait_send()
            third(j, part, 0).wait_send()

        @pl.when(core == 1)
        def _():
            pair(j, part, 1).wait_send()
            third(j, part, 1).wait_send()

    def chunk(j):
        def part(s, piece, pieces):
            size = width // pieces
            return xs.at[j, pl.ds(s * width + piece * size, size)]

        return part

    def sums(s, piece, pieces):
        size = n_slot // pieces
        return sb.at[s, pl.ds(piece * size, size)]

    def ring_up(buf, ss, rr, t):
        at = lax.rem(row + 2 * ROWS - t, ROWS)
        return remote(buf.at[at], buf.at[at], ss.at[t], rr.at[t], up)

    def ring_down(buf, ss, rr, t):
        at = lax.rem(row + t, ROWS)
        return remote(buf.at[at], buf.at[at], ss.at[4 + t], rr.at[4 + t], down)

    def ring_start(buf, ss, rr, t):
        ring_up(buf, ss, rr, t).start()
        if t < 3:
            ring_down(buf, ss, rr, t).start()

    def ring_recv(buf, ss, rr, t):
        ring_up(buf, ss, rr, t).wait_recv()
        if t < 3:
            ring_down(buf, ss, rr, t).wait_recv()

    cg[row] = coup[...]
    for j in range(CHUNKS):
        pltpu.make_async_copy(orb_hbm.at[:, pl.ds(j * cw, cw)], xs.at[j, pl.ds(0, width)], orb_sem.at[j]).wait()
        start_item(j, chunk(j))
    ring_start(cg, cy_s, cy_r, 0)

    for j in range(CHUNKS):
        pltpu.make_async_copy(proj_hbm.at[:, pl.ds(j * cw, cw)], pj.at[j], proj_sem.at[j]).wait()
        term = dot(pj[j], xs[j, 0:width, :], ((1,), (1,)))
        if j == 0:
            q32[:, 0:width] = term
        else:
            q32[:, 0:width] += term
    for p in range(0, n_proj, 2):
        even = q32[pl.ds(p, n_slot, stride=n_proj), :]
        odd = q32[pl.ds(p + 1, n_slot, stride=n_proj), :]
        both = jnp.concatenate([even[:, 0:width], odd[:, 0:width]], axis=1)
        g[row, :, p * width : (p + 2) * width] = both.astype(BF16)

    ring_start(g, y_s, y_r, 0)

    targets = jnp.concatenate([slot[pl.ds(c * ROWS + row, 1), :] for c in range(COLS)], axis=1)
    targets = jnp.broadcast_to(targets, (COLS * n_slot, COLS * n_slot)).T
    sources = jnp.concatenate([slot[pl.ds(col * ROWS + r, 1), :] for r in range(ROWS)], axis=1)
    n_tgt = COLS * n_slot
    pick = jnp.concatenate(
        [
            jnp.where(targets == jnp.broadcast_to(sources[:, i * n_tgt : (i + 1) * n_tgt], (n_tgt, n_tgt)), 1.0, 0.0)
            for i in range(2)
        ],
        axis=1,
    ).astype(BF16)
    atoms = coup.shape[0] * ROWS
    pick_atom = jnp.where(targets == col * atoms + lax.broadcasted_iota(jnp.int32, (n_tgt, atoms), 1), 1.0, 0.0)

    lane = lax.broadcasted_iota(jnp.int32, (4 * width, 4 * width), 1) // width
    sub = lax.broadcasted_iota(jnp.int32, (4 * width, 4 * width), 0) // width
    for s in range(4):
        tile = rot[:, s * width : (s + 1) * width].astype(F32)
        wide = jnp.concatenate([tile] * 4, axis=1)
        tall = jnp.concatenate([wide] * 4, axis=0)
        kr[s] = jnp.where(lane == sub, tall, 0.0).astype(BF16)

    for t in range(3):
        ring_recv(cg, cy_s, cy_r, t)
        ring_start(cg, cy_s, cy_r, t + 1)
        ring_recv(g, y_s, y_r, t)
        ring_start(g, y_s, y_r, t + 1)
        forward_item(t, chunk(t))
    ring_recv(cg, cy_s, cy_r, 3)

    def x_copy(k):
        to = lax.rem(col + k, COLS)
        return remote(xsend.at[to], xrecv.at[k], x_s.at[k], x_r.at[k], across(k))

    def cx_copy(k):
        to = lax.rem(col + k, COLS)
        return remote(csend.at[to], crecv.at[k], cx_s.at[k], cx_r.at[k], across(k))

    chosen = dot(pick_atom, cg[...].reshape(atoms, coup.shape[1]), ((1,), (0,)), HIGH)
    for c in range(COLS):
        csend[c] = chosen[c * n_slot : (c + 1) * n_slot]
    for k in range(1, COLS):
        cx_copy(k).start()

    ring_recv(g, y_s, y_r, 3)
    gathered = g[...].reshape(ROWS * n_slot, n_proj * width)
    combined = dot(pick, gathered, ((1,), (0,)))
    for c in range(COLS):
        xsend[c] = combined[c * n_slot : (c + 1) * n_slot].astype(BF16)
    for k in range(1, COLS):
        x_copy(k).start()
    forward_item(3, chunk(3))

    for k in range(1, COLS):
        cx_copy(k).wait_recv()
    mine = csend[col] + crecv[1] + crecv[2] + crecv[3]
    for p in range(n_proj):
        crow[pl.ds(p, n_slot, stride=n_proj), 0:n_proj] = mine[:, p * n_proj : (p + 1) * n_proj]
    reps = 256 // n_proj
    spread = jnp.where(
        lax.rem(lax.broadcasted_iota(jnp.int32, (n_proj, 256), 1), n_proj)
        == lax.broadcasted_iota(jnp.int32, (n_proj, 256), 0),
        1.0,
        0.0,
    )
    for i in range(2):
        wide = dot(crow[i * 256 : (i + 1) * 256, 0:n_proj], spread, ((1,), (0,)), HIGH)
        keep = (
            lax.broadcasted_iota(jnp.int32, (256, 256), 0) // n_proj
            == lax.broadcasted_iota(jnp.int32, (256, 256), 1) // n_proj
        )
        bd[i] = jnp.where(keep, wide, 0.0)

    for k in range(1, COLS):
        x_copy(k).wait_recv()
    total = xsend[col].astype(F32) + xrecv[1].astype(F32) + xrecv[2].astype(F32) + xrecv[3].astype(F32)
    sb[0] = total.astype(BF16)
    start_item(CHUNKS, sums)
    forward_item(4, chunk(4))
    forward_item(5, chunk(5))
    forward_item(CHUNKS, sums)
    finish_item(CHUNKS, sums)

    acc = None
    for s in range(4):
        block = sb[s]
        rows = jnp.concatenate([block[:, i * 256 : (i + 1) * 256] for i in range(4)], axis=0)
        term = dot(rows, kr[s], ((1,), (1,)))
        acc = term if acc is None else acc + term
    for p in range(n_proj):
        i, m = p // 4, p % 4
        s32[pl.ds(p, n_slot, stride=n_proj), 0:width] = acc[i * n_slot : (i + 1) * n_slot, m * width : (m + 1) * width]
    for i in range(2):
        coupled = dot(bd[i], s32[i * 256 : (i + 1) * 256, 0:width], ((1,), (0,)), HIGH)
        ct[:, i * 256 : (i + 1) * 256] = coupled.T.astype(BF16)

    for j in range(CHUNKS):
        finish_item(j, chunk(j))
        rotated = dot(rot[...], xs[j], ((1,), (0,))).astype(BF16)
        applied = dot(ct[...], pj[j], ((1,), (0,)))
        outv[j] = (rotated.astype(F32) + applied).astype(BF16)
        pltpu.make_async_copy(outv.at[j], out_hbm.at[:, pl.ds(j * cw, cw)], out_sem.at[j]).start()

    for j in range(CHUNKS):
        drain_item(j, chunk(j))
    drain_item(CHUNKS, sums)
    for t in range(4):
        for buf, ss, rr in ((cg, cy_s, cy_r), (g, y_s, y_r)):
            ring_up(buf, ss, rr, t).wait_send()
            if t < 3:
                ring_down(buf, ss, rr, t).wait_send()
    for k in range(1, COLS):
        x_copy(k).wait_send()
        cx_copy(k).wait_send()
    for j in range(CHUNKS):
        pltpu.make_async_copy(outv.at[j], out_hbm.at[:, pl.ds(j * cw, cw)], out_sem.at[j]).wait()


def on_device(orbitals, rotation, projectors, coupling, slot_atom):
    width, grid = orbitals.shape
    slots, n_proj, _ = projectors.shape
    cw = grid // CHUNKS
    pairs = slots * n_proj
    owned = coupling.shape[0]
    dma = pltpu.SemaphoreType.DMA
    items = CHUNKS + 1
    return pl.pallas_call(
        kernel,
        out_shape=jax.ShapeDtypeStruct((width, grid), BF16),
        in_specs=[
            pl.BlockSpec(memory_space=ANY),
            pl.BlockSpec(memory_space=VMEM),
            pl.BlockSpec(memory_space=ANY),
            pl.BlockSpec(memory_space=VMEM),
            pl.BlockSpec(memory_space=VMEM),
        ],
        out_specs=pl.BlockSpec(memory_space=ANY),
        scratch_shapes=[
            VMEM((CHUNKS, 4 * width, cw), BF16),
            VMEM((CHUNKS, pairs, cw), BF16),
            VMEM((pairs, 128), F32),
            VMEM((ROWS, slots, n_proj * width), BF16),
            VMEM((ROWS, owned, n_proj * n_proj), F32),
            VMEM((COLS, slots, n_proj * width), BF16),
            VMEM((COLS, slots, n_proj * width), BF16),
            VMEM((COLS, slots, n_proj * n_proj), F32),
            VMEM((COLS, slots, n_proj * n_proj), F32),
            VMEM((4, slots, n_proj * width), BF16),
            VMEM((4, 4 * width, 4 * width), BF16),
            VMEM((2, 256, 256), F32),
            VMEM((pairs, 128), F32),
            VMEM((pairs, 128), F32),
            VMEM((width, pairs), BF16),
            VMEM((CHUNKS, width, cw), BF16),
            dma((CHUNKS,)), dma((CHUNKS,)), dma((CHUNKS,)),
            dma((items,)), dma((items,)), dma((items,)), dma((items,)),
            dma((items,)), dma((items,)), dma((items,)), dma((items, 2)),
            dma((7,)), dma((7,)), dma((7,)), dma((7,)),
            dma((COLS,)), dma((COLS,)), dma((COLS,)), dma((COLS,)),
        ],
        compiler_params=pltpu.CompilerParams(
            collective_id=0, has_side_effects=True, vmem_limit_bytes=48 * 1024 * 1024
        ),
        name="exchange_and_apply",
    )(
        orbitals,
        rotation,
        projectors.reshape(pairs, grid),
        coupling.reshape(owned, n_proj * n_proj),
        slot_atom,
    )


def solution(mesh):
    in_specs = (P("band", "dom"), P("band", None), P(None, None, "dom"), P("dom", None, None), P())
    out_specs = P("band", "dom")
    return jax.shard_map(
        on_device, mesh=mesh, in_specs=in_specs, out_specs=out_specs, check_vma=False
    )
```

time: 433 us -> 100 us (0.23)
  the two profiles are of different devices: /device:TPU:16 before, /device:TPU:6 now
where the time goes in v1:
time: 100 us
  Pallas kernels  95.6 us (96%)
  local copies, waits for them, and re-layouts  4.49 us (4%)
    pallas_call x1, Pallas kernels, on_device(): pl.pallas_call(kernel, out_shape=jax.ShapeDtypeStruct((width, grid), BF16...  95.6 us
    unnamed x7, local copies, waits for them, and re-layouts  3.48 us

profile of v1, /device:TPU:6, one launch (start us, length us, event | category | flops | bytes accessed | tf_op | source)
XLA Modules:
  0.0 100.1 jit_solution(1210103843886187567)
XLA Ops:
  0.0 1.0 %reshape.7.coup = f32[16,256]{1,0:T(8,128)S(1)} reshape(f32[16,16,16]{2,1,0:T(8,128)} %param.8) | data formatting | bytes 32768 | tf_op jit(solution)/shard_map/reshape | solution.py:351
  1.0 0.0 copy-start
  1.0 1.1 %copy-done = bf16[64,6144]{1,0:T(8,128)(2,1)S(1)} copy-done((bf16[64,6144]{1,0:T(8,128)(2,1)S(1)}, bf16[64,6144]{1,0:T(8,128)(2,1)}, u32[]{:S(2)}) %copy-start) | copy-done | bytes 786456
  2.1 0.0 copy-start.1
  2.1 0.8 copy-done.1
  2.9 0.0 copy-start.2
  2.9 0.7 copy-done.2
  3.6 95.6 %exchange_and_apply.1 = bf16[64,6144]{1,0:T(8,128)(2,1)S(1)} custom-call(bf16[64,6144]{1,0:T(8,128)(2,1)S(1)} %copy-done, bf16[64,256]{1,0:T(8,128)(2,1)S(1)} %copy-done.1, bf16[512,6144]{1,0:T(8,128)(2,1)} %bitcast.1, f32[16,256]{1,0:T(8,128)S(1)} %reshape.7.coup, s32[32,32]{1,0:T(8,128)S(1)} %copy-done.2), custom_call_target="tpu_custom_call" | custom-call | tf_op jit(solution)/shard_map/exchange_and_apply/pallas_call | solution.py:309
  99.2 0.9 copy.7
Async XLA Ops:
  1.0 1.1 %copy-start = (bf16[64,6144]{1,0:T(8,128)(2,1)S(1)}, bf16[64,6144]{1,0:T(8,128)(2,1)}, u32[]{:S(2)}) copy-start(bf16[64,6144]{1,0:T(8,128)(2,1)} %orb_hbm.1) | copy-start | bytes 2359300
  2.1 0.8 copy-start.1
  2.9 0.7 copy-start.2

commit v2 on v1

v2 whole, which is shorter than its diff:
```python
import functools

import jax
import jax.numpy as jnp
from jax import lax
from jax.experimental import pallas as pl
from jax.experimental.pallas import tpu as pltpu
from jax.sharding import PartitionSpec as P

MESH = pl.DeviceIdType.MESH
HBM = pltpu.MemorySpace.HBM
VMEM = pltpu.VMEM
F32 = jnp.float32
BF16 = jnp.bfloat16
HIGH = lax.Precision.HIGHEST

CHUNKS = 6
COLS, ROWS = 4, 8
LEVELS = 8


def dot(a, b, dims, precision=None):
    return lax.dot_general(a, b, (dims, ((), ())), precision=precision, preferred_element_type=F32)


def kernel(
    orb_hbm, rot_hbm, proj_hbm, coup_hbm, slot_hbm, out_hbm,
    rot, coup, slot, hop, far, xs, pj, q32, g, cg, xsend, xrecv, csend, crecv, sb, kr, bd, crow, s32, ct, outv,
    small_sem, orb_sem, proj_sem, out_sem,
    link_s, link_r, pair_s, pair_r, own_s, own_r, third_s, third_r,
    relay_s, relay_r, give_s, give_r, cross_s, cross_r, down_s, down_r, last_s,
    y_s, y_r, x_s, x_r, cx_s, cx_r,
):
    band = lax.axis_index("band")
    dom = lax.axis_index("dom")
    n_band = lax.axis_size("band")
    core = lax.rem(band, 2)
    col, row = dom // ROWS, lax.rem(dom, ROWS)
    width = rot.shape[0]
    cw = xs.shape[2]
    n_slot = slot.shape[1]
    n_proj = coup.shape[1]

    first = band - core
    level = lax.rem(band // 2, LEVELS)
    last, lead = level == LEVELS - 1, level == 0
    top, middle = level == 6, level == 3
    opposite = (lax.rem(band + n_band // 2, n_band), dom)
    wrap = (lax.select(last, band - 2 * (LEVELS - 1), band + 2 * (LEVELS - 1)), dom)
    below = lax.rem(band + n_band - 6, n_band)
    above = lax.rem(band + 6, n_band)
    nxt = lax.rem(first + 2, n_band)
    prv = lax.rem(first + n_band - 2, n_band)
    partner = (first + 1 - core, dom)
    ahead = (nxt + core, dom)
    ahead0 = (nxt, dom)
    up = (band, col * ROWS + lax.rem(row + 1, ROWS))
    down = (band, col * ROWS + lax.rem(row + ROWS - 1, ROWS))

    def across(k):
        return (band, lax.rem(col + k, COLS) * ROWS + row)

    smalls = [
        pltpu.make_async_copy(coup_hbm, coup, small_sem.at[0]),
        pltpu.make_async_copy(slot_hbm, slot, small_sem.at[1]),
        pltpu.make_async_copy(rot_hbm, rot, small_sem.at[2]),
    ]
    for copy in smalls:
        copy.start()
    for j in range(CHUNKS):
        pltpu.make_async_copy(orb_hbm.at[:, pl.ds(j * cw, cw)], xs.at[j, pl.ds(0, width)], orb_sem.at[j]).start()
    def load_proj(h, j):
        half = proj_hbm.shape[0] // 2
        rows = pl.ds(h * half, half)
        return pltpu.make_async_copy(proj_hbm.at[rows, pl.ds(j * cw, cw)], pj.at[j, rows], proj_sem.at[h, j])

    for h in range(2):
        for j in range(CHUNKS):
            load_proj(h, j).start()

    barrier = pltpu.get_barrier_semaphore()

    def greet(friend):
        pl.semaphore_signal(barrier, inc=1, device_id=friend, device_id_type=MESH)

    for friend in (partner, (prv + core, dom), up, down, across(1), across(2), across(3), opposite):
        greet(friend)

    @pl.when(core == 0)
    def _():
        greet((prv + 1, dom))

    @pl.when(middle)
    def _():
        greet((above, dom))

    @pl.when(lead)
    def _():
        greet(wrap)

        @pl.when(core == 0)
        def _():
            greet((above, dom))
            greet((above + 1, dom))

    pl.semaphore_wait(barrier, 8 + core + lax.select(last | top | middle, 1, 0))

    def remote(src, dst, s, r, to):
        return pltpu.make_async_remote_copy(
            src_ref=src, dst_ref=dst, send_sem=s, recv_sem=r, device_id=to, device_id_type=MESH
        )

    def link(j, part, h):
        return remote(part(0, h, 2), part(2, h, 2), link_s.at[j, h], link_r.at[j, h], ahead)

    def own(j, part):
        return remote(part(0, 0, 1), part(1, 0, 1), own_s.at[j], own_r.at[j], partner)

    def pair(j, part, c):
        return remote(part(2, 0, 1), part(3 if c == 0 else 1, 0, 1), pair_s.at[j], pair_r.at[j], partner)

    def third(j, part, c):
        return remote(part(1 + c, c, 2), part(3, c, 2), third_s.at[j], third_r.at[j, c], ahead0)

    def relay_in(j):
        return remote(chunk(j)(0, 1, 2), hop.at[j], relay_s.at[j], relay_r.at[j], wrap)

    def relay_out(j):
        return remote(hop.at[j], chunk(j)(2, 1, 2), relay_s.at[j], link_r.at[j, 1], opposite)

    def give(j):
        return remote(chunk(j)(0, 1, 2), hop.at[j], give_s.at[j], give_r.at[j], partner)

    def cross(j, src):
        dst = far if j % 2 == 0 else hop
        return remote(src, dst.at[j], cross_s.at[j], cross_r.at[j], opposite)

    def fall(j, src):
        dst = hop if j % 2 == 0 else far
        return remote(src, dst.at[j], down_s.at[j], down_r.at[j], (below, dom))

    def land(j, c):
        h = 1 - c
        return remote(hop.at[j], chunk(j)(3, h, 2), last_s.at[j], third_r.at[j, h], (below - core, dom))

    def leave(j, src):
        (cross if j % 2 == 0 else fall)(j, src).start()

    def start_chunks():
        @pl.when(top & (core == 1))
        def _():
            for j in range(CHUNKS):
                give(j).start()

        @pl.when(jnp.logical_not(last) & (core == 0))
        def _():
            for j in range(CHUNKS):
                own(j, chunk(j)).start()

        @pl.when(last)
        def _():
            for j in range(CHUNKS):
                link(j, chunk(j), 0).start()
                relay_in(j).start()

        @pl.when(last & (core == 0))
        def _():
            for j in range(CHUNKS):
                own(j, chunk(j)).start()

        @pl.when(jnp.logical_not(last))
        def _():
            for j in range(CHUNKS):
                link(j, chunk(j), 0).start()
                link(j, chunk(j), 1).start()

        @pl.when(top & (core == 1))
        def _():
            for j in range(CHUNKS):
                leave(j, chunk(j)(0, 0, 2))

    def start_sums():
        link(CHUNKS, sums, 0).start()
        link(CHUNKS, sums, 1).start()

        @pl.when(core == 0)
        def _():
            own(CHUNKS, sums).start()

    def pump_give(j):
        @pl.when(top & (core == 0))
        def _():
            give(j).wait_recv()
            leave(j, hop.at[j])

    def pump_top(j):
        @pl.when(top)
        def _():
            cross(j, hop.at[j]).wait_recv()
            fall(j, far.at[j]).start()

    def pump_cross(j):
        @pl.when(middle)
        def _():
            fall(j, far.at[j]).wait_recv()
            cross(j, far.at[j]).start()

    def pump_land(j):
        @pl.when(middle)
        def _():
            (fall if j % 2 == 0 else cross)(j, far.at[j]).wait_recv()

            @pl.when(core == 0)
            def _():
                land(j, 0).start()

            @pl.when(core == 1)
            def _():
                land(j, 1).start()

    def pump_lead(j):
        @pl.when(lead)
        def _():
            relay_in(j).wait_recv()
            relay_out(j).start()

    def forward_item(j, part):
        link(j, part, 0).wait_recv()
        link(j, part, 1).wait_recv()

        @pl.when(core == 0)
        def _():
            pair(j, part, 0).start()

        @pl.when(core == 1)
        def _():
            pair(j, part, 1).start()

            @pl.when(jnp.logical_not(last) if j < CHUNKS else level >= 0)
            def _():
                third(j, part, 1).start()

    def pass_item(j, part):
        @pl.when(core == 0)
        def _():
            pair(j, part, 1).wait_recv()

            @pl.when(jnp.logical_not(last) if j < CHUNKS else level >= 0)
            def _():
                third(j, part, 0).start()

    def finish_item(j, part):
        @pl.when(core == 0)
        def _():
            third(j, part, 0).wait_recv()
            third(j, part, 1).wait_recv()

        @pl.when(core == 1)
        def _():
            own(j, part).wait_recv()
            pair(j, part, 0).wait_recv()

    def drain_item(j, part):
        link(j, part, 0).wait_send()
        passes = jnp.logical_not(last) if j < CHUNKS else level >= 0

        @pl.when(passes)
        def _():
            link(j, part, 1).wait_send()
            third(j, part, 0).wait_send()

        pair(j, part, 0).wait_send()

        @pl.when(core == 0)
        def _():
            own(j, part).wait_send()

    def drain_ways(j):
        @pl.when(last)
        def _():
            relay_in(j).wait_send()

        @pl.when(lead)
        def _():
            relay_out(j).wait_send()

        @pl.when(top)
        def _():
            @pl.when(core == 1)
            def _():
                give(j).wait_send()

            if j % 2 == 0:
                cross(j, hop.at[j]).wait_send()
            fall(j, far.at[j]).wait_send()

        @pl.when(middle)
        def _():
            if j % 2 == 1:
                cross(j, far.at[j]).wait_send()
            land(j, 0).wait_send()

    def chunk(j):
        def part(s, piece, pieces):
            size = width // pieces
            return xs.at[j, pl.ds(s * width + piece * size, size)]

        return part

    def sums(s, piece, pieces):
        size = n_slot // pieces
        return sb.at[s, pl.ds(piece * size, size)]

    hs = n_slot // 2

    def ring_copy(i, t, way):
        at = lax.rem(row + 2 * ROWS - way * t, ROWS)
        view = cg.at[at] if i == 0 else g.at[i - 1, at]
        n = t if way == 1 else 4 + t
        return remote(view, view, y_s.at[i, n], y_r.at[i, n], up if way == 1 else down)

    def ring_start(i, t):
        ring_copy(i, t, 1).start()
        if t < 3:
            ring_copy(i, t, -1).start()

    def ring_recv(i, t):
        ring_copy(i, t, 1).wait_recv()
        if t < 3:
            ring_copy(i, t, -1).wait_recv()

    for j in range(CHUNKS):
        pltpu.make_async_copy(orb_hbm.at[:, pl.ds(j * cw, cw)], xs.at[j, pl.ds(0, width)], orb_sem.at[j]).wait()
    start_chunks()

    for copy in smalls:
        copy.wait()
    for p in range(n_proj):
        cg[row, :, p * n_proj : (p + 1) * n_proj] = coup[:, p, :]
    ring_start(0, 0)
    for j in range(CHUNKS):
        pump_give(j)

    for h in range(2):
        rows = pl.ds(h * hs * n_proj, hs * n_proj)
        term = None
        for j in range(CHUNKS):
            load_proj(h, j).wait()
            more = dot(pj[j, rows, :], xs[j, 0:width, :], ((1,), (1,)))
            term = more if term is None else term + more
        q32[rows, 0:width] = term
        for p in range(0, n_proj, 2):
            even = q32[pl.ds(h * hs * n_proj + p, hs, stride=n_proj), :]
            odd = q32[pl.ds(h * hs * n_proj + p + 1, hs, stride=n_proj), :]
            both = jnp.concatenate([even[:, 0:width], odd[:, 0:width]], axis=1)
            g[h, row, :, p * width : (p + 2) * width] = both.astype(BF16)
        ring_start(1 + h, 0)

    targets = jnp.concatenate([slot[pl.ds(c * ROWS + row, 1), :] for c in range(COLS)], axis=1)
    targets = jnp.broadcast_to(targets, (COLS * n_slot, COLS * n_slot)).T
    n_tgt = COLS * n_slot
    near = [slot[pl.ds(col * ROWS + r, 1), :] for r in range(ROWS)]
    picks = []
    for h in range(2):
        sources = jnp.concatenate([line[:, h * hs : (h + 1) * hs] for line in near], axis=1)
        picks.append(jnp.where(targets == jnp.broadcast_to(sources, (n_tgt, n_tgt)), 1.0, 0.0).astype(BF16))
    atoms = coup.shape[0] * ROWS
    pick_atom = jnp.where(targets == col * atoms + lax.broadcasted_iota(jnp.int32, (n_tgt, atoms), 1), 1.0, 0.0)

    lane = lax.broadcasted_iota(jnp.int32, (4 * width, 4 * width), 1) // width
    sub = lax.broadcasted_iota(jnp.int32, (4 * width, 4 * width), 0) // width
    for s in range(4):
        tile = rot[:, s * width : (s + 1) * width].astype(F32)
        wide = jnp.concatenate([tile] * 4, axis=1)
        tall = jnp.concatenate([wide] * 4, axis=0)
        kr[s] = jnp.where(lane == sub, tall, 0.0).astype(BF16)

    for t in range(3):
        for i in range(3):
            ring_recv(i, t)
            ring_start(i, t + 1)
        pump_top(2 * t)
    ring_recv(0, 3)

    def x_copy(k):
        to = lax.rem(col + k, COLS)
        return remote(xsend.at[to], xrecv.at[k], x_s.at[k], x_r.at[k], across(k))

    def cx_copy(k):
        to = lax.rem(col + k, COLS)
        return remote(csend.at[to], crecv.at[k], cx_s.at[k], cx_r.at[k], across(k))

    chosen = dot(pick_atom, cg[...].reshape(atoms, n_proj * n_proj), ((1,), (0,)), HIGH)
    for c in range(COLS):
        csend[c] = chosen[c * n_slot : (c + 1) * n_slot]
    for k in range(1, COLS):
        cx_copy(k).start()

    combined = None
    for h in range(2):
        ring_recv(1 + h, 3)
        term = dot(picks[h], g[h].reshape(ROWS * hs, n_proj * width), ((1,), (0,)))
        combined = term if combined is None else combined + term
    for c in range(COLS):
        xsend[c] = combined[c * n_slot : (c + 1) * n_slot].astype(BF16)
    for k in range(1, COLS):
        x_copy(k).start()
    for k in range(1, COLS):
        cx_copy(k).wait_recv()
    mine = csend[col] + crecv[1] + crecv[2] + crecv[3]
    for p in range(n_proj):
        crow[pl.ds(p, n_slot, stride=n_proj), 0:n_proj] = mine[:, p * n_proj : (p + 1) * n_proj]
    reps = 256 // n_proj
    spread = jnp.where(
        lax.rem(lax.broadcasted_iota(jnp.int32, (n_proj, 256), 1), n_proj)
        == lax.broadcasted_iota(jnp.int32, (n_proj, 256), 0),
        1.0,
        0.0,
    )
    for i in range(2):
        wide = dot(crow[i * 256 : (i + 1) * 256, 0:n_proj], spread, ((1,), (0,)), HIGH)
        keep = (
            lax.broadcasted_iota(jnp.int32, (256, 256), 0) // n_proj
            == lax.broadcasted_iota(jnp.int32, (256, 256), 1) // n_proj
        )
        bd[i] = jnp.where(keep, wide, 0.0)

    for j in range(1, CHUNKS, 2):
        pump_cross(j)
    for k in range(1, COLS):
        x_copy(k).wait_recv()
    total = xsend[col].astype(F32) + xrecv[1].astype(F32) + xrecv[2].astype(F32) + xrecv[3].astype(F32)
    sb[0] = total.astype(BF16)
    start_sums()

    @pl.when(jnp.logical_not(lead))
    def _():
        for j in range(CHUNKS):
            forward_item(j, chunk(j))
        forward_item(CHUNKS, sums)

    for j in (1, 0, 3, 2, 5, 4):
        pump_land(j)

    @pl.when(jnp.logical_not(lead))
    def _():
        for j in range(CHUNKS):
            pass_item(j, chunk(j))
        pass_item(CHUNKS, sums)

    @pl.when(lead)
    def _():
        for j in range(3):
            pump_lead(j)
        for j in range(CHUNKS):
            forward_item(j, chunk(j))
            if j + 3 < CHUNKS:
                pump_lead(j + 3)
            if j >= 2:
                pass_item(j - 2, chunk(j - 2))
        for j in range(CHUNKS - 2, CHUNKS):
            pass_item(j, chunk(j))

    for j in range(CHUNKS):
        finish_item(j, chunk(j))
        outv[j] = dot(rot[...], xs[j], ((1,), (0,))).astype(BF16)

    @pl.when(lead)
    def _():
        forward_item(CHUNKS, sums)
        pass_item(CHUNKS, sums)

    for j in range(CHUNKS):
        drain_item(j, chunk(j))
        drain_ways(j)
    for i in range(3):
        for t in range(4):
            ring_copy(i, t, 1).wait_send()
            if t < 3:
                ring_copy(i, t, -1).wait_send()
    for k in range(1, COLS):
        x_copy(k).wait_send()
        cx_copy(k).wait_send()
    finish_item(CHUNKS, sums)

    acc = None
    for s in range(4):
        block = sb[s]
        rows = jnp.concatenate([block[:, i * 256 : (i + 1) * 256] for i in range(4)], axis=0)
        term = dot(rows, kr[s], ((1,), (1,)))
        acc = term if acc is None else acc + term
    for p in range(n_proj):
        i, m = p // 4, p % 4
        s32[pl.ds(p, n_slot, stride=n_proj), 0:width] = acc[i * n_slot : (i + 1) * n_slot, m * width : (m + 1) * width]
    for i in range(2):
        coupled = dot(bd[i], s32[i * 256 : (i + 1) * 256, 0:width], ((1,), (0,)), HIGH)
        ct[:, i * 256 : (i + 1) * 256] = coupled.T.astype(BF16)

    for j in range(CHUNKS):
        applied = dot(ct[...], pj[j], ((1,), (0,)))
        outv[j] = (outv[j].astype(F32) + applied).astype(BF16)
        pltpu.make_async_copy(outv.at[j], out_hbm.at[:, pl.ds(j * cw, cw)], out_sem.at[j]).start()

    drain_item(CHUNKS, sums)
    for j in range(CHUNKS):
        pltpu.make_async_copy(outv.at[j], out_hbm.at[:, pl.ds(j * cw, cw)], out_sem.at[j]).wait()


def on_device(orbitals, rotation, projectors, coupling, slot_atom):
    width, grid = orbitals.shape
    slots, n_proj, _ = projectors.shape
    cw = grid // CHUNKS
    pairs = slots * n_proj
    owned = coupling.shape[0]
    dma = pltpu.SemaphoreType.DMA
    items = CHUNKS + 1
    return pl.pallas_call(
        kernel,
        out_shape=jax.ShapeDtypeStruct((width, grid), BF16),
        in_specs=[pl.BlockSpec(memory_space=HBM)] * 5,
        out_specs=pl.BlockSpec(memory_space=HBM),
        scratch_shapes=[
            VMEM((width, 4 * width), BF16),
            VMEM(coupling.shape, F32),
            VMEM(slot_atom.shape, jnp.int32),
            VMEM((CHUNKS, width // 2, cw), BF16),
            VMEM((CHUNKS, width // 2, cw), BF16),
            VMEM((CHUNKS, 4 * width, cw), BF16),
            VMEM((CHUNKS, pairs, cw), BF16),
            VMEM((pairs, 128), F32),
            VMEM((2, ROWS, slots // 2, n_proj * width), BF16),
            VMEM((ROWS, owned, n_proj * n_proj), F32),
            VMEM((COLS, slots, n_proj * width), BF16),
            VMEM((COLS, slots, n_proj * width), BF16),
            VMEM((COLS, slots, n_proj * n_proj), F32),
            VMEM((COLS, slots, n_proj * n_proj), F32),
            VMEM((4, slots, n_proj * width), BF16),
            VMEM((4, 4 * width, 4 * width), BF16),
            VMEM((2, 256, 256), F32),
            VMEM((pairs, 128), F32),
            VMEM((pairs, 128), F32),
            VMEM((width, pairs), BF16),
            VMEM((CHUNKS, width, cw), BF16),
            dma((3,)), dma((CHUNKS,)), dma((2, CHUNKS)), dma((CHUNKS,)),
            dma((items, 2)), dma((items, 2)), dma((items,)), dma((items,)),
            dma((items,)), dma((items,)), dma((items,)), dma((items, 2)),
            *[dma((CHUNKS,))] * 9,
            dma((3, 7)), dma((3, 7)),
            dma((COLS,)), dma((COLS,)), dma((COLS,)), dma((COLS,)),
        ],
        compiler_params=pltpu.CompilerParams(
            collective_id=0, has_side_effects=True, vmem_limit_bytes=67_043_328
        ),
        name="exchange_and_apply",
    )(
        orbitals,
        rotation,
        projectors.reshape(pairs, grid),
        coupling,
        slot_atom,
    )


def solution(mesh):
    in_specs = (P("band", "dom"), P("band", None), P(None, None, "dom"), P("dom", None, None), P())
    out_specs = P("band", "dom")
    return jax.shard_map(
        on_device, mesh=mesh, in_specs=in_specs, out_specs=out_specs, check_vma=False
    )
```

time: 100 us -> 74.6 us (0.75)
  Pallas kernels: 95.6 us -> 72.4 us
  local copies, waits for them, and re-layouts: 4.49 us -> 2.06 us
    pallas_call x1, Pallas kernels: 95.6 us -> 72.4 us  [on_device(): pl.pallas_call(kernel, out_shape=jax.ShapeDtypeStruct((width, grid), BF16...]
    unnamed x7 -> x1, local copies, waits for them, and re-layouts: 3.48 us -> 2.06 us
    reshape x1 -> x0, local copies, waits for them, and re-layouts: 1.01 us -> none  [on_device(): coupling.reshape(owned, n_proj * n_proj)]
where the time goes in v2:
time: 74.6 us; the launch traced here: 74.4 us
  Pallas kernels  72.4 us (97%)
  local copies, waits for them, and re-layouts  2.06 us (3%)
    pallas_call x1, Pallas kernels, on_device(): pl.pallas_call(kernel, out_shape=jax.ShapeDtypeStruct((width, grid), BF16...  72.4 us
    unnamed x1, local copies, waits for them, and re-layouts  2.06 us

profile of v2, /device:TPU:6, one launch (start us, length us, event | category | flops | bytes accessed | tf_op | source)
XLA Modules:
  0.0 74.4 jit_solution(7424624097331519704)
XLA Ops:
  0.0 72.4 %exchange_and_apply.1 = bf16[64,6144]{1,0:T(8,128)(2,1)} custom-call(bf16[64,6144]{1,0:T(8,128)(2,1)} %orb_hbm.1, bf16[64,256]{1,0:T(8,128)(2,1)} %rot_hbm.1, bf16[512,6144]{1,0:T(8,128)(2,1)} %bitcast.1, f32[16,16,16]{2,1,0:T(8,128)} %coup_hbm.1, s32[32,32]{1,0:T(8,128)} %slot_hbm.1), custom_call_target="tpu_custom_call" | custom-call | tf_op jit(solution)/shard_map/exchange_and_apply/pallas_call | solution.py:517
  72.4 2.1 %copy.7 = bf16[64,6144]{1,0:T(8,128)(2,1)} copy(bf16[64,6144]{1,0:T(8,128)(2,1)} %exchange_and_apply.1) | data formatting | bytes 1572864

commit v3 on v2

--- a/solution.py
+++ b/solution.py
@@ -17,6 +17,8 @@
 CHUNKS = 6
 COLS, ROWS = 4, 8
 LEVELS = 8
+EARLY = 3
+SIDE = 3
 
 
 def dot(a, b, dims, precision=None):
@@ -25,10 +27,10 @@
 
 def kernel(
     orb_hbm, rot_hbm, proj_hbm, coup_hbm, slot_hbm, out_hbm,
-    rot, coup, slot, hop, far, xs, pj, q32, g, cg, xsend, xrecv, csend, crecv, sb, kr, bd, crow, s32, ct, outv,
+    rot, coup, slot, hop, far, side, xs, pj, q32, g, cg, xsend, xrecv, csend, crecv, sb, kr, bd, crow, s32, ct, outv,
     small_sem, orb_sem, proj_sem, out_sem,
     link_s, link_r, pair_s, pair_r, own_s, own_r, third_s, third_r,
-    relay_s, relay_r, give_s, give_r, cross_s, cross_r, down_s, down_r, last_s,
+    side_s, side_r, relay_s, relay_r, give_s, give_r, cross_s, cross_r, down_s, down_r, last_s,
     y_s, y_r, x_s, x_r, cx_s, cx_r,
 ):
     band = lax.axis_index("band")
@@ -44,9 +46,10 @@
     first = band - core
     level = lax.rem(band // 2, LEVELS)
     last, lead = level == LEVELS - 1, level == 0
-    top, middle = level == 6, level == 3
+    top, middle, second = level == 6, level == 3, level == 1
     opposite = (lax.rem(band + n_band // 2, n_band), dom)
     wrap = (lax.select(last, band - 2 * (LEVELS - 1), band + 2 * (LEVELS - 1)), dom)
+    far_side = lax.rem(band + n_band // 2, n_band)
     below = lax.rem(band + n_band - 6, n_band)
     above = lax.rem(band + 6, n_band)
     nxt = lax.rem(first + 2, n_band)
@@ -94,16 +97,26 @@
     def _():
         greet((above, dom))
 
+    @pl.when(top)
+    def _():
+        greet((band + 2, dom))
+
+    @pl.when(second)
+    def _():
+        greet((band + 12, dom))
+
     @pl.when(lead)
     def _():
         greet(wrap)
+        greet((far_side + 2, dom))
+        greet((far_side + 12, dom))
 
         @pl.when(core == 0)
         def _():
             greet((above, dom))
             greet((above + 1, dom))
 
-    pl.semaphore_wait(barrier, 8 + core + lax.select(last | top | middle, 1, 0))
+    pl.semaphore_wait(barrier, 8 + core + lax.select(last, 3, lax.select(top, 2, lax.select(middle | second, 1, 0))))
 
     def remote(src, dst, s, r, to):
         return pltpu.make_async_remote_copy(
@@ -120,13 +133,35 @@
         return remote(part(2, 0, 1), part(3 if c == 0 else 1, 0, 1), pair_s.at[j], pair_r.at[j], partner)
 
     def third(j, part, c):
+        if j == CHUNKS:
+            return remote(part(2, 0, 1), part(3, 0, 1), third_s.at[j], third_r.at[j, c], ahead0)
         return remote(part(1 + c, c, 2), part(3, c, 2), third_s.at[j], third_r.at[j, c], ahead0)
 
     def relay_in(j):
-        return remote(chunk(j)(0, 1, 2), hop.at[j], relay_s.at[j], relay_r.at[j], wrap)
+        to = wrap if j < SIDE else (band - 12, dom)
+        return remote(chunk(j)(0, 1, 2), hop.at[j], relay_s.at[j], relay_r.at[j], to)
 
     def relay_out(j):
-        return remote(hop.at[j], chunk(j)(2, 1, 2), relay_s.at[j], link_r.at[j, 1], opposite)
+        to = opposite if j < SIDE else (far_side - 2, dom)
+        return remote(hop.at[j], chunk(j)(2, 1, 2), relay_s.at[j], link_r.at[j, 1], to)
+
+    def side_in(j):
+        return remote(chunk(j)(0, 0, 2), side.at[j - SIDE], side_s.at[j], side_r.at[j], (band - 2, dom))
+
+    def side_out(j):
+        return remote(side.at[j - SIDE], chunk(j)(2, 0, 2), side_s.at[j], link_r.at[j, 0], (far_side - 12, dom))
+
+    def pump_side(j):
+        @pl.when(top)
+        def _():
+            side_in(j).wait_recv()
+            side_out(j).start()
+
+    def pump_second(j):
+        @pl.when(second)
+        def _():
+            relay_in(j).wait_recv()
+            relay_out(j).start()
 
     def give(j):
         return remote(chunk(j)(0, 1, 2), hop.at[j], give_s.at[j], give_r.at[j], partner)
@@ -159,14 +194,12 @@
 
         @pl.when(last)
         def _():
-            for j in range(CHUNKS):
+            for j in range(SIDE, CHUNKS):
+                side_in(j).start()
+                relay_in(j).start()
+            for j in range(SIDE):
                 link(j, chunk(j), 0).start()
                 relay_in(j).start()
-
-        @pl.when(last & (core == 0))
-        def _():
-            for j in range(CHUNKS):
-                own(j, chunk(j)).start()
 
         @pl.when(jnp.logical_not(last))
         def _():
@@ -234,25 +267,24 @@
 
         @pl.when(core == 1)
         def _():
+            if j == CHUNKS:
+                third(j, part, 1).start()
             pair(j, part, 1).start()
-
-            @pl.when(jnp.logical_not(last) if j < CHUNKS else level >= 0)
-            def _():
-                third(j, part, 1).start()
+            if j < CHUNKS:
+                pl.when(jnp.logical_not(last))(third(j, part, 1).start)
 
     def pass_item(j, part):
         @pl.when(core == 0)
         def _():
             pair(j, part, 1).wait_recv()
-
-            @pl.when(jnp.logical_not(last) if j < CHUNKS else level >= 0)
-            def _():
-                third(j, part, 0).start()
+            if j < CHUNKS:
+                pl.when(jnp.logical_not(last))(third(j, part, 0).start)
 
     def finish_item(j, part):
         @pl.when(core == 0)
         def _():
-            third(j, part, 0).wait_recv()
+            if j < CHUNKS:
+                third(j, part, 0).wait_recv()
             third(j, part, 1).wait_recv()
 
         @pl.when(core == 1)
@@ -261,15 +293,21 @@
             pair(j, part, 0).wait_recv()
 
     def drain_item(j, part):
-        link(j, part, 0).wait_send()
-        passes = jnp.logical_not(last) if j < CHUNKS else level >= 0
-
-        @pl.when(passes)
-        def _():
+        if j < SIDE or j == CHUNKS:
+            link(j, part, 0).wait_send()
+        else:
+            pl.when(jnp.logical_not(last))(link(j, part, 0).wait_send)
+        pair(j, part, 0).wait_send()
+        if j < CHUNKS:
+
+            @pl.when(jnp.logical_not(last))
+            def _():
+                link(j, part, 1).wait_send()
+                third(j, part, 0).wait_send()
+
+        else:
             link(j, part, 1).wait_send()
-            third(j, part, 0).wait_send()
-
-        pair(j, part, 0).wait_send()
+            pl.when(core == 1)(third(j, part, 1).wait_send)
 
         @pl.when(core == 0)
         def _():
@@ -279,8 +317,10 @@
         @pl.when(last)
         def _():
             relay_in(j).wait_send()
-
-        @pl.when(lead)
+            if j >= SIDE:
+                side_in(j).wait_send()
+
+        @pl.when(lead if j < SIDE else second)
         def _():
             relay_out(j).wait_send()
 
@@ -293,6 +333,8 @@
             if j % 2 == 0:
                 cross(j, hop.at[j]).wait_send()
             fall(j, far.at[j]).wait_send()
+            if j >= SIDE:
+                side_out(j).wait_send()
 
         @pl.when(middle)
         def _():
@@ -376,12 +418,11 @@
         kr[s] = jnp.where(lane == sub, tall, 0.0).astype(BF16)
 
     for t in range(3):
-        for i in range(3):
+        for i in (1, 2, 0):
             ring_recv(i, t)
             ring_start(i, t + 1)
         pump_top(2 * t)
-    ring_recv(0, 3)
-
+        pump_side(SIDE + t)
     def x_copy(k):
         to = lax.rem(col + k, COLS)
         return remote(xsend.at[to], xrecv.at[k], x_s.at[k], x_r.at[k], across(k))
@@ -389,12 +430,6 @@
     def cx_copy(k):
         to = lax.rem(col + k, COLS)
         return remote(csend.at[to], crecv.at[k], cx_s.at[k], cx_r.at[k], across(k))
-
-    chosen = dot(pick_atom, cg[...].reshape(atoms, n_proj * n_proj), ((1,), (0,)), HIGH)
-    for c in range(COLS):
-        csend[c] = chosen[c * n_slot : (c + 1) * n_slot]
-    for k in range(1, COLS):
-        cx_copy(k).start()
 
     combined = None
     for h in range(2):
@@ -405,6 +440,14 @@
         xsend[c] = combined[c * n_slot : (c + 1) * n_slot].astype(BF16)
     for k in range(1, COLS):
         x_copy(k).start()
+
+    ring_recv(0, 3)
+    chosen = dot(pick_atom, cg[...].reshape(atoms, n_proj * n_proj), ((1,), (0,)), HIGH)
+    for c in range(COLS):
+        csend[c] = chosen[c * n_slot : (c + 1) * n_slot]
+    for k in range(1, COLS):
+        cx_copy(k).start()
+
     for k in range(1, COLS):
         cx_copy(k).wait_recv()
     mine = csend[col] + crecv[1] + crecv[2] + crecv[3]
@@ -427,12 +470,21 @@
 
     for j in range(1, CHUNKS, 2):
         pump_cross(j)
+    for j in range(SIDE, CHUNKS):
+        pump_second(j)
+    for j in range(EARLY):
+        pump_lead(j)
     for k in range(1, COLS):
         x_copy(k).wait_recv()
     total = xsend[col].astype(F32) + xrecv[1].astype(F32) + xrecv[2].astype(F32) + xrecv[3].astype(F32)
     sb[0] = total.astype(BF16)
     start_sums()
 
+    @pl.when(last & (core == 0))
+    def _():
+        for j in range(CHUNKS):
+            own(j, chunk(j)).start()
+
     @pl.when(jnp.logical_not(lead))
     def _():
         for j in range(CHUNKS):
@@ -450,12 +502,10 @@
 
     @pl.when(lead)
     def _():
-        for j in range(3):
-            pump_lead(j)
         for j in range(CHUNKS):
             forward_item(j, chunk(j))
-            if j + 3 < CHUNKS:
-                pump_lead(j + 3)
+            if j + EARLY < SIDE:
+                pump_lead(j + EARLY)
             if j >= 2:
                 pass_item(j - 2, chunk(j - 2))
         for j in range(CHUNKS - 2, CHUNKS):
@@ -525,6 +575,7 @@
             VMEM(slot_atom.shape, jnp.int32),
             VMEM((CHUNKS, width // 2, cw), BF16),
             VMEM((CHUNKS, width // 2, cw), BF16),
+            VMEM((CHUNKS - SIDE, width // 2, cw), BF16),
             VMEM((CHUNKS, 4 * width, cw), BF16),
             VMEM((CHUNKS, pairs, cw), BF16),
             VMEM((pairs, 128), F32),
@@ -544,7 +595,7 @@
             dma((3,)), dma((CHUNKS,)), dma((2, CHUNKS)), dma((CHUNKS,)),
             dma((items, 2)), dma((items, 2)), dma((items,)), dma((items,)),
             dma((items,)), dma((items,)), dma((items,)), dma((items, 2)),
-            *[dma((CHUNKS,))] * 9,
+            *[dma((CHUNKS,))] * 11,
             dma((3, 7)), dma((3, 7)),
             dma((COLS,)), dma((COLS,)), dma((COLS,)), dma((COLS,)),
         ],

time: 74.6 us -> 69.3 us (0.929)
  the two profiles are of different devices: /device:TPU:6 before, /device:TPU:3 now
where the time goes in v3:
time: 69.3 us; the launch traced here: 69.2 us
  Pallas kernels  67.1 us (97%)
  local copies, waits for them, and re-layouts  2.06 us (3%)
    pallas_call x1, Pallas kernels, on_device(): pl.pallas_call(kernel, out_shape=jax.ShapeDtypeStruct((width, grid), BF16...  67.1 us
    unnamed x1, local copies, waits for them, and re-layouts  2.06 us

profile of v3, /device:TPU:3, one launch (start us, length us, event | category | flops | bytes accessed | tf_op | source)
XLA Modules:
  0.0 69.2 jit_solution(15668431836896747395)
XLA Ops:
  0.0 67.1 %exchange_and_apply.1 = bf16[64,6144]{1,0:T(8,128)(2,1)} custom-call(bf16[64,6144]{1,0:T(8,128)(2,1)} %orb_hbm.1, bf16[64,256]{1,0:T(8,128)(2,1)} %rot_hbm.1, bf16[512,6144]{1,0:T(8,128)(2,1)} %bitcast.1, f32[16,16,16]{2,1,0:T(8,128)} %coup_hbm.1, s32[32,32]{1,0:T(8,128)} %slot_hbm.1), custom_call_target="tpu_custom_call" | custom-call | tf_op jit(solution)/shard_map/exchange_and_apply/pallas_call | solution.py:567
  67.1 2.1 %copy.7 = bf16[64,6144]{1,0:T(8,128)(2,1)} copy(bf16[64,6144]{1,0:T(8,128)(2,1)} %exchange_and_apply.1) | data formatting | bytes 1572864

commit v4 on v3

--- a/solution.py
+++ b/solution.py
@@ -480,6 +480,10 @@
     sb[0] = total.astype(BF16)
     start_sums()
 
+    @pl.when(last)
+    def _():
+        forward_item(CHUNKS, sums)
+
     @pl.when(last & (core == 0))
     def _():
         for j in range(CHUNKS):
@@ -489,6 +493,9 @@
     def _():
         for j in range(CHUNKS):
             forward_item(j, chunk(j))
+
+    @pl.when(jnp.logical_not(lead) & jnp.logical_not(last))
+    def _():
         forward_item(CHUNKS, sums)
 
     for j in (1, 0, 3, 2, 5, 4):
@@ -520,9 +527,6 @@
         forward_item(CHUNKS, sums)
         pass_item(CHUNKS, sums)
 
-    for j in range(CHUNKS):
-        drain_item(j, chunk(j))
-        drain_ways(j)
     for i in range(3):
         for t in range(4):
             ring_copy(i, t, 1).wait_send()
@@ -551,6 +555,9 @@
         outv[j] = (outv[j].astype(F32) + applied).astype(BF16)
         pltpu.make_async_copy(outv.at[j], out_hbm.at[:, pl.ds(j * cw, cw)], out_sem.at[j]).start()
 
+    for j in range(CHUNKS):
+        drain_item(j, chunk(j))
+        drain_ways(j)
     drain_item(CHUNKS, sums)
     for j in range(CHUNKS):
         pltpu.make_async_copy(outv.at[j], out_hbm.at[:, pl.ds(j * cw, cw)], out_sem.at[j]).wait()

time: 69.3 us -> 69.3 us (level)
  no operation moved by 1% of the time
where the time goes in v4:
time: 69.3 us; the launch traced here: 69.2 us
  Pallas kernels  67.1 us (97%)
  local copies, waits for them, and re-layouts  2.06 us (3%)
    pallas_call x1, Pallas kernels, on_device(): pl.pallas_call(kernel, out_shape=jax.ShapeDtypeStruct((width, grid), BF16...  67.1 us
    unnamed x1, local copies, waits for them, and re-layouts  2.06 us

profile of v4, /device:TPU:3, one launch (start us, length us, event | category | flops | bytes accessed | tf_op | source)
XLA Modules:
  0.0 69.2 jit_solution(9400208653716230080)
XLA Ops:
  0.0 67.1 %exchange_and_apply.1 = bf16[64,6144]{1,0:T(8,128)(2,1)} custom-call(bf16[64,6144]{1,0:T(8,128)(2,1)} %orb_hbm.1, bf16[64,256]{1,0:T(8,128)(2,1)} %rot_hbm.1, bf16[512,6144]{1,0:T(8,128)(2,1)} %bitcast.1, f32[16,16,16]{2,1,0:T(8,128)} %coup_hbm.1, s32[32,32]{1,0:T(8,128)} %slot_hbm.1), custom_call_target="tpu_custom_call" | custom-call | tf_op jit(solution)/shard_map/exchange_and_apply/pallas_call | solution.py:574
  67.1 2.1 %copy.7 = bf16[64,6144]{1,0:T(8,128)(2,1)} copy(bf16[64,6144]{1,0:T(8,128)(2,1)} %exchange_and_apply.1) | data formatting | bytes 1572864
